TPU v7x, 256 devices: a whole 4x4x8 slice. The times are simulated.
256 devices in a mesh: seq: 32 (over y, z), dp: 8 (over x, core).
Axes of the slice: x: 4, y: 4, z: 8, core: 2. Of those that a mesh axis runs over, the one named last changes fastest.
Arguments:
- frames: bfloat16 [32, 4096, 384], P('dp', 'seq'), may hold values from -48 to 48
- w_query: bfloat16 [384, 384], replicated, may hold values from -0.3125 to 0.3125
- w_key: bfloat16 [384, 384], replicated, may hold values from -0.3125 to 0.3125
- w_value: bfloat16 [384, 384], replicated, may hold values from -0.3125 to 0.3125
- w_out: bfloat16 [384, 384], replicated, may hold values from -0.3125 to 0.3125
- valid_counts: int32 [32, 128], P('dp', 'seq'), may hold values from 1 to 32
- out_grad: bfloat16 [32, 4096, 384], P('dp', 'seq'), may hold values from -6 to 6
Outputs:
- attended: bfloat16 [32, 4096, 384], P('dp', 'seq')
- frame_grads: bfloat16 [32, 4096, 384], P('dp', 'seq')
- weight_grads: float32 [4, 384, 384], replicated
Inputs may be any that keep to these rules, and one draw needn't show every extreme that they name: `valid_counts`: valid frames of each span, counted from the span's start.
All inputs are finite; a program needn't handle non-finite values.
Results may differ from a plain program's by a relative error of at most 0.013.
The roundings to bfloat16 on the way count: a program that leaves them out, or rounds other values in their place, can miss the bound.
Values may be sent and summed in bfloat16 or wider, within the bound.
No kernel may reach another device: no remote copies, remote signals or barrier semaphores. Data moves between devices by JAX's collectives and lax.ppermute only.
A program may use at most 64 MiB of HBM per device.

v0:
```python
from functools import partial

import jax
import jax.numpy as jnp
from jax import lax
from jax.sharding import PartitionSpec as P

HEADS = 4
CH = 32
CTX = 128


def shifted(value, axis, by):
    length = lax.axis_size(axis)
    pairs = [(i, i + by) for i in range(length) if 0 <= i + by < length]
    return lax.ppermute(value, axis, pairs)


def windows(padded, nch, wide, ch):
    blocks = padded.reshape((nch + wide - 1, ch) + padded.shape[1:])
    return jnp.concatenate([blocks[i : i + nch] for i in range(wide)], 1)


def unwindow(win, nch, wide, ch):
    rest = win.shape[2:]
    total = jnp.zeros((nch + wide - 1, ch) + rest, win.dtype)
    for i in range(wide):
        total = total.at[i : i + nch].add(win[:, i * ch : (i + 1) * ch])
    return total.reshape(((nch + wide - 1) * ch,) + rest)


def project(data, weight):
    return jnp.dot(data, weight, preferred_element_type=jnp.float32).astype(jnp.bfloat16)


def backdot(data, weight):
    return lax.dot_general(
        data, weight, (((1,), (1,)), ((), ())), preferred_element_type=jnp.float32
    )


def coldot(left, right):
    return lax.dot_general(
        left, right, (((0,), (0,)), ((), ())), preferred_element_type=jnp.float32
    )


def forward_one(query, key_pad, value_pad, ok_pad, heads, ch, ctx):
    local, width = query.shape
    nch = local // ch
    wide = ctx // ch + 1
    size = width // heads
    scale = size ** (-0.5)
    qc = query.reshape(nch, ch, heads, size)
    kw = windows(key_pad, nch, wide, ch).reshape(nch, wide * ch, heads, size)
    vw = windows(value_pad, nch, wide, ch).reshape(nch, wide * ch, heads, size)
    okw = windows(ok_pad, nch, wide, ch)
    scores = jnp.einsum("cqhe,ckhe->chqk", qc, kw, preferred_element_type=jnp.float32) * scale
    scores = jnp.where(okw[:, None, None, :], scores, jnp.float32(-1e30))
    top = jnp.max(scores, -1, keepdims=True)
    expo = jnp.exp(scores - top)
    probs = expo / jnp.sum(expo, -1, keepdims=True)
    probs_b = probs.astype(jnp.bfloat16)
    context = jnp.einsum("chqk,ckhe->cqhe", probs_b, vw, preferred_element_type=jnp.float32)
    return (probs, probs_b, context.astype(jnp.bfloat16).reshape(local, width))


def backward_one(query, key_pad, value_pad, probs, probs_b, d_context, heads, ch, ctx):
    local, width = query.shape
    nch = local // ch
    wide = ctx // ch + 1
    size = width // heads
    scale = size ** (-0.5)
    qc = query.reshape(nch, ch, heads, size)
    kw = windows(key_pad, nch, wide, ch).reshape(nch, wide * ch, heads, size)
    vw = windows(value_pad, nch, wide, ch).reshape(nch, wide * ch, heads, size)
    dc = d_context.reshape(nch, ch, heads, size)
    d_probs = jnp.einsum("cqhe,ckhe->chqk", dc, vw, preferred_element_type=jnp.float32)
    delta = jnp.sum(probs * d_probs, -1, keepdims=True)
    d_scores = (probs * (d_probs - delta) * scale).astype(jnp.bfloat16)
    d_query = jnp.einsum("chqk,ckhe->cqhe", d_scores, kw, preferred_element_type=jnp.float32)
    d_kw = jnp.einsum("chqk,cqhe->ckhe", d_scores, qc, preferred_element_type=jnp.float32).reshape(
        nch, wide * ch, width
    )
    d_vw = jnp.einsum("chqk,cqhe->ckhe", probs_b, dc, preferred_element_type=jnp.float32).reshape(
        nch, wide * ch, width
    )
    return (
        d_query.astype(jnp.bfloat16).reshape(local, width),
        unwindow(d_kw, nch, wide, ch),
        unwindow(d_vw, nch, wide, ch),
    )


def body(frames, w_query, w_key, w_value, w_out, valid_counts, out_grad):
    batch, local, width = frames.shape
    rows = frames.reshape(batch * local, width)
    query = project(rows, w_query).reshape(batch, local, width)
    keys = project(rows, w_key).reshape(batch, local, width)
    values = project(rows, w_value).reshape(batch, local, width)
    prev_keys, prev_values, prev_counts = shifted((keys, values, valid_counts), "seq", 1)
    key_pad = jnp.concatenate([prev_keys, keys], 1)
    value_pad = jnp.concatenate([prev_values, values], 1)
    count_pad = jnp.concatenate([prev_counts, valid_counts], 1)
    slots = lax.broadcasted_iota(jnp.int32, (1, 1, CH), 2)
    ok_pad = (slots < count_pad[:, :, None]).reshape(batch, CTX + local)
    forward = jax.vmap(partial(forward_one, heads=HEADS, ch=CH, ctx=CTX))
    probs, probs_b, context = forward(query, key_pad, value_pad, ok_pad)
    context_rows = context.reshape(batch * local, width)
    attended = project(context_rows, w_out).reshape(batch, local, width)
    grad_rows = out_grad.reshape(batch * local, width)
    d_context = backdot(grad_rows, w_out).astype(jnp.bfloat16).reshape(batch, local, width)
    backward = jax.vmap(partial(backward_one, heads=HEADS, ch=CH, ctx=CTX))
    d_query, d_key_pad, d_value_pad = backward(query, key_pad, value_pad, probs, probs_b, d_context)
    back_key, back_value = shifted((d_key_pad[:, :CTX], d_value_pad[:, :CTX]), "seq", -1)
    own_key = d_key_pad[:, CTX:]
    own_value = d_value_pad[:, CTX:]
    d_key = jnp.concatenate([own_key[:, : local - CTX], own_key + back_key], 1).astype(jnp.bfloat16)
    d_value = jnp.concatenate([own_value[:, : local - CTX], own_value + back_value], 1).astype(
        jnp.bfloat16
    )
    dq_rows = d_query.reshape(batch * local, width)
    dk_rows = d_key.reshape(batch * local, width)
    dv_rows = d_value.reshape(batch * local, width)
    frame_grads = (
        backdot(dq_rows, w_query) + backdot(dk_rows, w_key) + backdot(dv_rows, w_value)
    ).astype(jnp.bfloat16)
    partial_grads = jnp.stack(
        [
            coldot(rows, dq_rows),
            coldot(rows, dk_rows),
            coldot(rows, dv_rows),
            coldot(context_rows, grad_rows),
        ]
    )
    weight_grads = lax.psum(partial_grads, ("seq", "dp"))
    return (attended, frame_grads.reshape(batch, local, width), weight_grads)


def solution(mesh):
    in_specs = (P("dp", "seq", None), P(), P(), P(), P(), P("dp", "seq"), P("dp", "seq", None))
    out_specs = (P("dp", "seq", None), P("dp", "seq", None), P())
    return jax.shard_map(body, mesh=mesh, in_specs=in_specs, out_specs=out_specs, check_vma=False)
```

profile of v0, /device:TPU:1, one launch (start us, length us, event | category | flops | bytes accessed | tf_op | source)
XLA Modules:
  0.0 448.8 jit_solution(16456905830640947338)
XLA Ops:
  7.3 4.5 %collective-permute-start.1 = (s32[4,4]{1,0:T(4,128)}, s32[4,4]{1,0:T(4,128)S(1)}, u32[]{:S(2)}, u32[]{:S(2)}) collective-permute-start(s32[4,4]{1,0:T(4,128)} %param.32), channel_id=1, source_target_pairs={{0,8},{8,16},{16,24},{24,32},{32,40},{40,48},{48,56},{56,64},{64,7... | collective-permute-start | bytes 200 | tf_op jit(solution)/shard_map/ppermute | solution.py:16
  11.8 2.1 convolution_convert_fusion.4
  13.9 4.3 collective-permute-start
  18.2 1.3 convolution_convert_fusion.2
  19.5 2.8 collective-permute-start.2
  23.6 1.2 reshape_reshape.7
  25.0 8.5 %collective-permute-done.2 = bf16[4,128,384]{2,1,0:T(8,128)(2,1)S(1)} collective-permute-done((bf16[4,128,384]{2,1,0:T(8,128)(2,1)S(1)}, bf16[4,128,384]{2,1,0:T(8,128)(2,1)S(1)}, u32[]{:S(2)}, u32[]{:S(2)}) %collective-permute-start.2) | collective-permute-done | bytes 393248 | tf_op jit(solution)/shard_map/ppermute | solution.py:16
  37.6 4.9 %reshape.409 = bf16[4,4,160,4,96]{4,3,2,1,0:T(4,128)(2,1)S(1)} reshape(bf16[4,4,160,384]{3,2,1,0:T(8,128)(2,1)} %slice_dynamic-update-slice_fusion.5) | data formatting | bytes 3932160 | tf_op jit(solution)/shard_map/vmap()/reshape | solution.py:55
  42.5 1.2 pad_maximum_fusion.2
  47.7 6.0 %reshape.406 = bf16[4,4,160,4,96]{4,3,2,1,0:T(4,128)(2,1)} reshape(bf16[4,4,160,384]{3,2,1,0:T(8,128)(2,1)} %slice_dynamic-update-slice_fusion) | data formatting | bytes 3932160 | tf_op jit(solution)/shard_map/vmap()/reshape | solution.py:56
  53.7 2.9 fusion.8
  56.6 3.1 fusion.2
  59.6 2.5 fusion.63
  62.1 6.9 %fusion.27 = bf16[4,4,32,4,96]{4,2,3,1,0:T(8,128)(2,1)} fusion(bf16[4,4,160,4,96]{4,3,2,1,0:T(4,128)(2,1)} %reshape.406, f32[4,4,4,32]{3,2,1,0:T(4,128)} %get-tuple-element.134, f32[4,4,4,32,160]{4,3,2,1,0:T(8,128)} %copy-done.4, pred[4,4,160]{2,1,0:T(4,128)(4,1)S(1)} %concatenate.43), kind=kOutput, calls=%fused_computation.33 | convolution fusion | flops 64751776 | bytes 3680768 | tf_op jit(solution)/shard_map/vmap(chqk,ckhe->cqhe)/dot_general | solution.py:64
  69.0 15.6 %fusion.30 = bf16[4,4,32,4,96]{4,2,3,1,0:T(8,128)(2,1)} fusion(bf16[4,4,160,4,96]{4,3,2,1,0:T(4,128)(2,1)S(1)} %reshape.409, f32[4,4,4,32,160]{4,3,2,1,0:T(8,128)} %fusion.2, f32[4,4,4,32,160]{4,3,2,1,0:T(8,128)} %get-tuple-element.135, f32[4,4,4,32]{3,2,1,0:T(4,128)} %get-tuple-element.134), kind=kOutput, calls=%fused_computation.34 | convolution fusion | flops 65407136 | bytes 4988928 | tf_op jit(solution)/shard_map/vmap(chqk,ckhe->cqhe)/dot_general | solution.py:81
  84.6 18.4 %convolution_bitcast_fusion.1 = f32[4,4,160,4,96]{4,2,3,1,0:T(8,128)} fusion(f32[4,4,4,32,160]{4,3,2,1,0:T(8,128)} %fusion.2, bf16[4,4,32,4,96]{4,3,2,1,0:T(4,128)(2,1)} %reshape_reshape.7, f32[4,4,4,32,160]{4,3,2,1,0:T(8,128)} %get-tuple-element.135, f32[4,4,4,32]{3,2,1,0:T(4,128)} %get-tuple-element.134), kind=kOutput, calls=%fused_computation.3 | convolution fusion | flops 65210528 | bytes 6955008 | tf_op jit(solution)/shard_map/vmap(chqk,cqhe->ckhe)/dot_general | solution.py:82
  103.0 8.6 %convolution_bitcast_fusion = f32[4,4,160,4,96]{4,2,3,1,0:T(8,128)} fusion(bf16[4,4,32,4,96]{4,3,2,1,0:T(4,128)(2,1)S(1)} %reshape_reshape.8, f32[4,4,4,32]{3,2,1,0:T(4,128)S(1)} %copy-done.15, f32[4,4,4,32,160]{4,3,2,1,0:T(8,128)} %copy-done.4, pred[4,4,160]{2,1,0:T(4,128)(4,1)S(1)} %concatenate.43), kind=kOutput, calls=%fused_computation.2 | convolution fusion | flops 64555168 | bytes 5646848 | tf_op jit(solution)/shard_map/vmap(chqk,cqhe->ckhe)/dot_general | solution.py:85
  113.3 8.3 %copy.25 = f32[4,4,160,4,96]{4,3,2,1,0:T(4,128)} copy(f32[4,4,160,4,96]{4,2,3,1,0:T(8,128)} %convolution_bitcast_fusion.1) | data formatting | bytes 7864320 | tf_op jit(solution)/shard_map/vmap(chqk,cqhe->ckhe)/transpose | solution.py:82
  121.6 6.5 %reshape.414 = f32[4,4,160,384]{3,2,1,0:T(8,128)} reshape(f32[4,4,160,4,96]{4,3,2,1,0:T(4,128)} %copy.25) | data formatting | bytes 7864320 | tf_op jit(solution)/shard_map/vmap()/reshape | solution.py:82
  129.5 1.5 fusion.49
  132.3 1.6 collective-permute-start.3
  133.9 5.8 %copy.27 = f32[4,4,160,4,96]{4,3,2,1,0:T(4,128)} copy(f32[4,4,160,4,96]{4,2,3,1,0:T(8,128)S(1)} %bitcast.85) | data formatting | bytes 7864320 | tf_op jit(solution)/shard_map/vmap(chqk,cqhe->ckhe)/transpose | solution.py:85
  139.7 6.5 %reshape.417 = f32[4,4,160,384]{3,2,1,0:T(8,128)} reshape(f32[4,4,160,4,96]{4,3,2,1,0:T(4,128)} %copy.27) | data formatting | bytes 7864320 | tf_op jit(solution)/shard_map/vmap()/reshape | solution.py:85
  147.5 1.5 fusion.44
  150.4 1.3 collective-permute-start.4
  152.5 1.2 fusion.45
  154.1 17.0 %collective-permute-done.4 = f32[4,128,384]{2,1,0:T(8,128)S(1)} collective-permute-done((f32[4,128,384]{2,1,0:T(8,128)S(1)}, f32[4,128,384]{2,1,0:T(8,128)S(1)}, u32[]{:S(2)}, u32[]{:S(2)}) %collective-permute-start.4) | collective-permute-done | bytes 786464 | tf_op jit(solution)/shard_map/ppermute | solution.py:16
  171.6 1.6 pad_maximum_fusion
  174.2 1.1 convolution_convert_fusion.1
  176.3 1.2 fusion.26
  177.4 261.5 %all-reduce.4.cloned.1.call-done = f32[4,384,384]{1,2,0:T(8,128)} async-done(((f32[4,384,384]{1,2,0:T(8,128)}), f32[4,384,384]{1,2,0:T(8,128)}) %all-reduce.4.cloned.1.call-update) | async-done | bytes 2359312 | tf_op jit(solution)/shard_map/psum | solution.py:136
  438.9 3.0 copy.31
  (87 shorter events, 20.0 us)
Async XLA Ops:
  7.2 4.6 %copy-start = (bf16[4,128,384]{2,1,0:T(8,128)(2,1)S(1)}, bf16[4,128,384]{2,1,0:T(8,128)(2,1)}, u32[]{:S(2)}) copy-start(bf16[4,128,384]{2,1,0:T(8,128)(2,1)} %param.27) | copy-start | bytes 1179652
  7.2 15.2 %copy-start.9 = (bf16[384,384]{1,0:T(8,128)(2,1)S(1)}, bf16[384,384]{1,0:T(8,128)(2,1)}, u32[]{:S(2)}) copy-start(bf16[384,384]{1,0:T(8,128)(2,1)} %param.31) | copy-start | bytes 884740
  7.2 15.2 %copy-start.5 = (bf16[4,128,384]{2,1,0:T(8,128)(2,1)S(1)}, bf16[4,128,384]{2,1,0:T(8,128)(2,1)}, u32[]{:S(2)}) copy-start(bf16[4,128,384]{2,1,0:T(8,128)(2,1)} %param.33) | copy-start | bytes 1179652
  7.2 16.0 %copy-start.11 = (bf16[384,384]{1,0:T(8,128)(2,1)S(1)}, bf16[384,384]{1,0:T(8,128)(2,1)}, u32[]{:S(2)}) copy-start(bf16[384,384]{1,0:T(8,128)(2,1)} %param.28) | copy-start | bytes 884740
  7.2 431.7 %all-reduce.4.cloned.1.call-start = ((), (), s32[]{:S(2)}) async-start(), calls=%async_computation | async-start | bytes 4718592 | tf_op jit(solution)/shard_map/psum | solution.py:136
  7.3 17.5 %collective-permute-start.1 = (s32[4,4]{1,0:T(4,128)}, s32[4,4]{1,0:T(4,128)S(1)}, u32[]{:S(2)}, u32[]{:S(2)}) collective-permute-start(s32[4,4]{1,0:T(4,128)} %param.32), channel_id=1, source_target_pairs={{0,8},{8,16},{16,24},{24,32},{32,40},{40,48},{48,56},{56,64},{64,7... | collective-permute-start | bytes 200 | tf_op jit(solution)/shard_map/ppermute | solution.py:16
  13.9 28.6 %collective-permute-start = (bf16[4,128,384]{2,1,0:T(8,128)(2,1)}, bf16[4,128,384]{2,1,0:T(8,128)(2,1)}, u32[]{:S(2)}, u32[]{:S(2)}) collective-permute-start(bf16[4,128,384]{2,1,0:T(8,128)(2,1)} %bitcast.1), channel_id=1, source_target_pairs={{0,8},{8,16},{16,24},{24,32},{32,40},{40,48},{48,56},{56,64},{64,7... | collective-permute-start | bytes 1179656 | tf_op jit(solution)/shard_map/ppermute | solution.py:16
  19.5 5.2 %copy-start.16 = (s32[4,4]{1,0:T(4,128)S(1)}, s32[4,4]{1,0:T(4,128)}, u32[]{:S(2)}) copy-start(s32[4,4]{1,0:T(4,128)} %param.32) | copy-start | bytes 196
  19.5 14.0 %collective-permute-start.2 = (bf16[4,128,384]{2,1,0:T(8,128)(2,1)S(1)}, bf16[4,128,384]{2,1,0:T(8,128)(2,1)S(1)}, u32[]{:S(2)}, u32[]{:S(2)}) collective-permute-start(bf16[4,128,384]{2,1,0:T(8,128)(2,1)S(1)} %bitcast.90), channel_id=1, source_target_pairs={{0,8},{8,16},{16,24},{24,32},{32,40},{40,48},{48,56},{56,64},{64,7... | collective-permute-start | bytes 1179656 | tf_op jit(solution)/shard_map/ppermute | solution.py:16
  53.7 2.9 copy-start.3
  56.5 3.1 copy-start.4
  84.6 18.4 %copy-start.15 = (f32[4,4,4,32]{3,2,1,0:T(4,128)S(1)}, f32[4,4,4,32]{3,2,1,0:T(4,128)}, u32[]{:S(2)}) copy-start(f32[4,4,4,32]{3,2,1,0:T(4,128)} %get-tuple-element.134) | copy-start | bytes 24580
  103.0 8.6 %copy-start.14 = (bf16[4,4,32,4,96]{4,2,3,1,0:T(8,128)(2,1)S(1)}, bf16[4,4,32,4,96]{4,2,3,1,0:T(8,128)(2,1)}, u32[]{:S(2)}) copy-start(bf16[4,4,32,4,96]{4,2,3,1,0:T(8,128)(2,1)} %fusion.30) | copy-start | bytes 1179652
  111.6 1.0 copy-start.13
  128.2 1.1 slice-start.1
  129.3 2.4 copy-start.2
  129.3 4.6 %slice-start.2 = ((s8[5242880]{0:T(1024)(128)(4,1)}), s8[4194304]{0:T(1024)(128)(4,1)S(1)}, s32[]{:S(2)}) async-start(s8[5242880]{0:T(1024)(128)(4,1)} %bitcast.84), calls=%async_computation.3 | async-start | bytes 8388608
  131.7 2.2 slice-start.3
  132.3 20.2 %collective-permute-start.3 = (f32[4,128,384]{2,1,0:T(8,128)S(1)}, f32[4,128,384]{2,1,0:T(8,128)}, u32[]{:S(2)}, u32[]{:S(2)}) collective-permute-start(f32[4,128,384]{2,1,0:T(8,128)S(1)} %slice.442), channel_id=1, source_target_pairs={{8,0},{16,8},{24,16},{32,24},{40,32},{48,40},{56,48},{64,56},{72,6... | collective-permute-start | bytes 2359304 | tf_op jit(solution)/shard_map/ppermute | solution.py:16
  146.2 1.1 slice-start
  147.4 2.4 copy-start.1
  150.1 1.6 copy-start.6
  150.4 20.7 %collective-permute-start.4 = (f32[4,128,384]{2,1,0:T(8,128)S(1)}, f32[4,128,384]{2,1,0:T(8,128)S(1)}, u32[]{:S(2)}, u32[]{:S(2)}) collective-permute-start(f32[4,128,384]{2,1,0:T(8,128)S(1)} %slice.452), channel_id=1, source_target_pairs={{8,0},{16,8},{24,16},{32,24},{40,32},{48,40},{56,48},{64,56},{72,6... | collective-permute-start | bytes 2359304 | tf_op jit(solution)/shard_map/ppermute | solution.py:16
  173.2 1.0 copy-start.10
  173.2 2.1 copy-start.12
  173.2 2.5 copy-start.7
  175.3 1.0 copy-start.8
Sparse Core Ops, SparseCore 0:
  173.4 265.4 all-reduce.3
where the time goes:
time: 451 us; the launch traced here: 449 us
  waiting for transfers between devices  287 us (64%)
  matrix products  64.4 us (14%)
  local copies, waits for them, and re-layouts  57.5 us (13%)
  starting transfers between devices  14.5 us (3%)
  between operations  14.4 us (3%)
  other arithmetic  11 us (2%)
    psum x1, waiting for transfers between devices, body(): weight_grads = lax.psum(partial_grads, ('seq', 'dp'))  261 us
    ppermute x5, waiting for transfers between devices, shifted(): return lax.ppermute(value, axis, pairs)  25.5 us
    dot_general x1, matrix products, backward_one(): jnp.einsum('chqk,cqhe->ckhe', d_scores, qc, preferred_element_type=jnp.fl...  18.4 us
    dot_general x1, matrix products, backward_one(): jnp.einsum('chqk,ckhe->cqhe', d_scores, kw, preferred_element_type=jnp.fl...  15.6 us
    ppermute x5, starting transfers between devices, shifted(): return lax.ppermute(value, axis, pairs)  14.5 us
    unnamed x47, local copies, waits for them, and re-layouts  12.3 us
  transfers between devices with their start and end apart: 6, of which 3 were waited for; matrix products, arithmetic and copies ran while one was open for 8% of the time, Pallas kernels for 0%

commit v1 on v0

v1 whole, which is shorter than its diff:
```python
import jax
import jax.numpy as jnp
from jax import lax
from jax.experimental import pallas as pl
from jax.experimental.pallas import tpu as pltpu
from jax.sharding import PartitionSpec as P

HEADS = 4
CH = 32
CTX = 128
LENGTH_Z = 8
CORES = 2
EVERY = ("seq", "dp")
BF16 = jnp.bfloat16
F32 = jnp.float32


def shifted(value, axis, by):
    length = lax.axis_size(axis)
    pairs = [(i, i + by) for i in range(length) if 0 <= i + by < length]
    return lax.ppermute(value, axis, pairs)


def plain(left, right):
    return jnp.dot(left, right, preferred_element_type=F32)


def rows_dot(left, right):
    return lax.dot_general(left, right, (((1,), (1,)), ((), ())), preferred_element_type=F32)


def cols_dot(left, right):
    return lax.dot_general(left, right, (((0,), (0,)), ((), ())), preferred_element_type=F32)


def attention_kernel(
    own_counts, prev_counts, core_ref, x_ref, xp_ref, g_ref, wq_ref, wk_ref, wv_ref, wo_ref,
    att_ref, fg_ref, fgp_ref, keep_ref, send_ref,
    q_s, k_s, v_s, dc_s, ctx_s, dq_s, dk_s, dv_s,
):
    batch, local, width = x_ref.shape
    size = width // HEADS
    scale = size ** (-0.5)
    keys = CTX + local
    many = HEADS * local
    rows = batch * local

    x = x_ref[...].reshape(rows, width)
    xp = xp_ref[...].reshape(rows, width)
    g = g_ref[...].reshape(rows, width)

    def spread(value):
        return value.astype(BF16).reshape(batch, local, width)

    q_s[...] = spread(plain(x, wq_ref[...]))
    dc_s[...] = spread(rows_dot(g, wo_ref[...]))
    k_s[:, CTX:, :] = spread(plain(x, wk_ref[...]))
    v_s[:, CTX:, :] = spread(plain(x, wv_ref[...]))
    k_s[:, :CTX, :] = spread(plain(xp, wk_ref[...]))
    v_s[:, :CTX, :] = spread(plain(xp, wv_ref[...]))

    head_of = lax.broadcasted_iota(jnp.int32, (local, width), 1) // size
    lane_span = (lax.broadcasted_iota(jnp.int32, (CH, many), 1) % local) // CH
    slot = lax.broadcasted_iota(jnp.int32, (CH, many), 0)

    def by_head(value):
        zero = jnp.zeros_like(value)
        return jnp.concatenate([jnp.where(head_of == h, value, zero) for h in range(HEADS)], 0)

    def own_head(wide):
        out = wide[:local]
        for h in range(1, HEADS):
            out = jnp.where(head_of == h, wide[h * local : (h + 1) * local], out)
        return out

    def one(u, carry):
        k = k_s[u]
        v = v_s[u]
        qm = by_head(q_s[u])
        dcm = by_head(dc_s[u])
        scores = rows_dot(k, qm)
        parts = []
        for s in range(keys // CH):
            count = prev_counts[u, s] if s < CTX // CH else own_counts[u, s - CTX // CH]
            behind = s - lane_span
            seen = (slot < count) & (behind >= 0) & (behind <= CTX // CH)
            parts.append(jnp.where(seen, scores[s * CH : (s + 1) * CH] * scale, F32(-1e30)))
        scores = jnp.concatenate(parts, 0)
        top = jnp.max(scores, 0, keepdims=True)
        expo = jnp.exp(scores - top)
        probs = expo * (1.0 / jnp.sum(expo, 0, keepdims=True))
        probs_b = probs.astype(BF16)
        ctx_s[u] = own_head(cols_dot(probs_b, v)).astype(BF16)
        d_probs = rows_dot(v, dcm)
        delta = jnp.sum(probs * d_probs, 0, keepdims=True)
        d_scores = (probs * (d_probs - delta) * scale).astype(BF16)
        dq_s[u] = own_head(cols_dot(d_scores, k)).astype(BF16)
        dk_s[u] = plain(d_scores, qm).astype(BF16)
        dv_s[u] = plain(probs_b, dcm).astype(BF16)
        return carry

    lax.fori_loop(0, batch, one, 0)

    ctx = ctx_s[...].reshape(rows, width)
    dq = dq_s[...].reshape(rows, width)
    dk = dk_s[:, CTX:, :].reshape(rows, width)
    dv = dv_s[:, CTX:, :].reshape(rows, width)
    dkp = dk_s[:, :CTX, :].reshape(rows, width)
    dvp = dv_s[:, :CTX, :].reshape(rows, width)

    att_ref[...] = spread(plain(ctx, wo_ref[...]))
    fgp_ref[...] = spread(rows_dot(dkp, wk_ref[...]) + rows_dot(dvp, wv_ref[...]))
    total = rows_dot(dq, wq_ref[...]) + rows_dot(dk, wk_ref[...]) + rows_dot(dv, wv_ref[...])
    fg_ref[...] = total.reshape(batch, local, width)
    grads = [
        cols_dot(x, dq),
        cols_dot(x, dk) + cols_dot(xp, dkp),
        cols_dot(x, dv) + cols_dot(xp, dvp),
        cols_dot(ctx, g),
    ]
    core = core_ref[0]

    @pl.when(core == 0)
    def _():
        for i in range(2):
            keep_ref[i] = grads[i]
            send_ref[i] = grads[2 + i]

    @pl.when(core != 0)
    def _():
        for i in range(2):
            keep_ref[i] = grads[2 + i]
            send_ref[i] = grads[i]


def attention(own_counts, prev_counts, core, x, xp, g, w_query, w_key, w_value, w_out):
    batch, local, width = x.shape
    smem = pl.BlockSpec(memory_space=pltpu.SMEM)
    vmem = pl.BlockSpec(memory_space=pltpu.VMEM)
    short = pltpu.VMEM((batch, local, width), BF16)
    long = pltpu.VMEM((batch, CTX + local, width), BF16)
    return pl.pallas_call(
        attention_kernel,
        out_shape=[
            jax.ShapeDtypeStruct((batch, local, width), BF16),
            jax.ShapeDtypeStruct((batch, local, width), F32),
            jax.ShapeDtypeStruct((batch, local, width), BF16),
            jax.ShapeDtypeStruct((2, width, width), F32),
            jax.ShapeDtypeStruct((2, width, width), F32),
        ],
        in_specs=[smem] * 3 + [vmem] * 7,
        out_specs=[vmem] * 5,
        scratch_shapes=[short, long, long, short, short, short, long, long],
        name="attention",
    )(own_counts, prev_counts, core, x, xp, g, w_query, w_key, w_value, w_out)


def groups():
    seq, dp = lax.axis_size("seq"), lax.axis_size("dp")
    z, c = min(LENGTH_Z, seq // 2), CORES
    y, x = seq // z, dp // c

    def at(iy, iz, ix, ic):
        return (iy * z + iz) * dp + ix * c + ic

    plane = [
        [at(iy, iz, ix, ic) for iy in range(y) for ix in range(x)] for iz in range(z) for ic in range(c)
    ]
    column = [
        [at(iy, iz, ix, ic) for iz in range(z)] for iy in range(y) for ix in range(x) for ic in range(c)
    ]
    return plane, column


def partner(value):
    pairs = [(i, i ^ 1) for i in range(lax.axis_size("dp"))]
    return lax.ppermute(value, "dp", pairs)


def exchange(value, members):
    return lax.all_to_all(value, EVERY, 0, 0, axis_index_groups=members)


def to_all(value, members):
    return exchange(jnp.broadcast_to(value[None], (len(members[0]),) + value.shape), members)


def add_up(pieces):
    return jnp.sum(pieces.astype(F32), 0).astype(BF16)


def total_grads(keep, send, core):
    plane, column = groups()
    half, width, _ = keep.shape
    mine = (keep + partner(send)).astype(BF16)
    mine = mine.reshape(len(plane[0]), half * width // len(plane[0]), width)
    mine = add_up(exchange(mine, plane))
    mine = add_up(to_all(mine, column))
    mine = to_all(mine, plane).reshape(half, width, width)
    other = partner(mine)
    first = jnp.where(core == 0, mine, other)
    second = jnp.where(core == 0, other, mine)
    return jnp.concatenate([first, second], 0).astype(F32)


def body(frames, w_query, w_key, w_value, w_out, valid_counts, out_grad):
    core = lax.axis_index("dp") % CORES
    prev_frames = shifted(frames, "seq", 1)
    prev_counts = shifted(valid_counts, "seq", 1)
    attended, own, back, keep, send = attention(
        valid_counts, prev_counts, core[None], frames, prev_frames, out_grad, w_query, w_key, w_value, w_out
    )
    returned = shifted(back, "seq", -1)
    weight_grads = total_grads(keep, send, core)
    frame_grads = (own + returned.astype(F32)).astype(BF16)
    return (attended, frame_grads, weight_grads)


def solution(mesh):
    in_specs = (P("dp", "seq", None), P(), P(), P(), P(), P("dp", "seq"), P("dp", "seq", None))
    out_specs = (P("dp", "seq", None), P("dp", "seq", None), P())
    return jax.shard_map(body, mesh=mesh, in_specs=in_specs, out_specs=out_specs, check_vma=False)
```

time: 451 us -> 93.9 us (0.21)
  waiting for transfers between devices: 287 us -> 16 us
  matrix products: 64.4 us -> 0 us
  local copies, waits for them, and re-layouts: 57.5 us -> 1.65 us
  blocking collectives: 0 us -> 37 us
  Pallas kernels: 0 us -> 14.2 us
  between operations: 14.4 us -> 0.71 us
  other arithmetic: 11 us -> 4.08 us
  starting transfers between devices: 14.5 us -> 19.8 us
    psum x1 -> x0, waiting for transfers between devices: 261 us -> none  [body(): weight_grads = lax.psum(partial_grads, ('seq', 'dp'))]
    dot_general x18 -> x0, matrix products: 64.4 us -> none  [the longest x1 18.4 us: backward_one(): jnp.einsum('chqk,cqhe->ckhe', d_scores, qc, preferred_element_type=jnp.fl...]
    all_to_all x0 -> x2, blocking collectives: none -> 37 us  [exchange(): return lax.all_to_all(value, EVERY, 0, 0, axis_index_groups=members)]
    reshape x6 -> x0, local copies, waits for them, and re-layouts: 24.7 us -> none  [the longest x1 6.53 us: backward_one(): jnp.einsum('chqk,cqhe->ckhe', probs_b, dc, preferred_element_type=jnp.flo...]
    ppermute x5 -> x3, waiting for transfers between devices: 25.5 us -> 4.52 us  [shifted(): return lax.ppermute(value, axis, pairs)]
    pallas_call x0 -> x1, Pallas kernels: none -> 14.2 us  [attention(): pl.pallas_call(attention_kernel, out_shape=[jax.ShapeDtypeStruct((batch,...]
    transpose x2 -> x0, local copies, waits for them, and re-layouts: 14.1 us -> none  [the longest x1 8.32 us: backward_one(): jnp.einsum('chqk,cqhe->ckhe', d_scores, qc, preferred_element_type=jnp.fl...]
    unnamed x47 -> x8, local copies, waits for them, and re-layouts: 12.3 us -> 0.75 us
  transfers between devices with their start and end apart: 6 -> 6, of which waited for: 3 -> 4; matrix products, arithmetic and copies ran while one was open for 8% -> 1% of each run, Pallas kernels for 0% -> 0%
where the time goes in v1:
time: 93.9 us; the launch traced here: 93.5 us
  blocking collectives  37 us (39%)
  starting transfers between devices  19.8 us (21%)
  waiting for transfers between devices  16 us (17%)
  Pallas kernels  14.2 us (15%)
  other arithmetic  4.08 us (4%)
  local copies, waits for them, and re-layouts  1.65 us (2%)
    all_to_all x2, blocking collectives, exchange(): return lax.all_to_all(value, EVERY, 0, 0, axis_index_groups=members)  37 us
    pallas_call x1, Pallas kernels, attention(): pl.pallas_call(attention_kernel, out_shape=[jax.ShapeDtypeStruct((batch,...  14.2 us
    ppermute x3, starting transfers between devices, shifted(): return lax.ppermute(value, axis, pairs)  9.21 us
    all_to_all x1, waiting for transfers between devices, exchange(): return lax.all_to_all(value, EVERY, 0, 0, axis_index_groups=members)  8.03 us
    ppermute x2, starting transfers between devices, partner(): return lax.ppermute(value, 'dp', pairs)  6.23 us
    ppermute x3, waiting for transfers between devices, shifted(): return lax.ppermute(value, axis, pairs)  4.52 us
    all_to_all x1, starting transfers between devices, exchange(): return lax.all_to_all(value, EVERY, 0, 0, axis_index_groups=members)  4.37 us
    ppermute x2, waiting for transfers between devices, partner(): return lax.ppermute(value, 'dp', pairs)  3.49 us
  transfers between devices with their start and end apart: 6, of which 4 were waited for; matrix products, arithmetic and copies ran while one was open for 1% of the time, Pallas kernels for 0%

profile of v1, /device:TPU:1, one launch (start us, length us, event | category | flops | bytes accessed | tf_op | source)
XLA Modules:
  0.0 93.5 jit_solution(4380064196464328798)
XLA Ops:
  0.6 4.4 %collective-permute-start.1 = (bf16[4,128,384]{2,1,0:T(8,128)(2,1)}, bf16[4,128,384]{2,1,0:T(8,128)(2,1)S(1)}, u32[]{:S(2)}, u32[]{:S(2)}) collective-permute-start(bf16[4,128,384]{2,1,0:T(8,128)(2,1)} %x_ref.1), channel_id=1, source_target_pairs={{0,8},{8,16},{16,24},{24,32},{32,40},{40,48},{48,56},{56,64},{64,7... | collective-permute-start | bytes 1179656 | tf_op jit(solution)/shard_map/ppermute | solution.py:21
  5.0 3.5 %collective-permute-start = (s32[4,4]{1,0:T(4,128)}, s32[4,4]{1,0:T(4,128)S(1)}, u32[]{:S(2)}, u32[]{:S(2)}) collective-permute-start(s32[4,4]{1,0:T(4,128)} %own_counts.1), channel_id=1, source_target_pairs={{0,8},{8,16},{16,24},{24,32},{32,40},{40,48},{48,56},{56,64},{64,7... | collective-permute-start | bytes 200 | tf_op jit(solution)/shard_map/ppermute | solution.py:21
  8.6 4.5 %collective-permute-done.prev_counts = s32[4,4]{1,0:T(4,128)S(1)} collective-permute-done((s32[4,4]{1,0:T(4,128)}, s32[4,4]{1,0:T(4,128)S(1)}, u32[]{:S(2)}, u32[]{:S(2)}) %collective-permute-start) | collective-permute-done | bytes 96 | tf_op jit(solution)/shard_map/ppermute | solution.py:21
  13.1 0.0 copy-start.2
  13.1 0.0 collective-permute-done.1.xp_ref
  13.1 0.0 copy-start.1
  13.1 0.6 copy-done.2
  13.7 0.2 copy-done.1
  13.8 14.2 %attention.1 = (bf16[4,128,384]{2,1,0:T(8,128)(2,1)}, f32[4,128,384]{2,1,0:T(8,128)}, bf16[4,128,384]{2,1,0:T(8,128)(2,1)}, f32[2,384,384]{2,1,0:T(8,128)}, f32[2,384,384]{2,1,0:T(8,128)}) custom-call(s32[4,4]{1,0:T(4,128)} %own_counts.1, s32[4,4]{1,0:T(4,128)} %copy-done.2, s32[1]{0:T(128)} %bitcast.core_ref, bf16[4,128,384]{2,1,0:T(8,128)(2,1)} %x_ref.1, ...), custom_call_target="tpu_custom_call" | custom-call | tf_op jit(solution)/shard_map/attention/pallas_call | solution.py:142
  28.1 1.6 %collective-permute-start.3 = (f32[2,384,384]{2,1,0:T(8,128)}, f32[2,384,384]{2,1,0:T(8,128)S(1)}, u32[]{:S(2)}, u32[]{:S(2)}) collective-permute-start(f32[2,384,384]{2,1,0:T(8,128)} %get-tuple-element.12), channel_id=1, source_target_pairs={{0,1},{1,0},{2,3},{3,2},{4,5},{5,4},{6,7},{7,6},{8,9},{9,8},{10,11... | collective-permute-start | bytes 3538952 | tf_op jit(solution)/shard_map/ppermute | solution.py:177
  29.6 2.7 %collective-permute-done.3 = f32[2,384,384]{2,1,0:T(8,128)S(1)} collective-permute-done((f32[2,384,384]{2,1,0:T(8,128)}, f32[2,384,384]{2,1,0:T(8,128)S(1)}, u32[]{:S(2)}, u32[]{:S(2)}) %collective-permute-start.3) | collective-permute-done | bytes 1179680 | tf_op jit(solution)/shard_map/ppermute | solution.py:177
  32.3 1.5 %add_convert_fusion = bf16[2,384,384]{2,1,0:T(8,128)(2,1)S(1)} fusion(f32[2,384,384]{2,1,0:T(8,128)} %get-tuple-element.11, f32[2,384,384]{2,1,0:T(8,128)S(1)} %collective-permute-done.3), kind=kLoop, calls=%fused_computation.1 | loop fusion | flops 589824 | bytes 2949120 | tf_op jit(solution)/shard_map/convert_element_type | solution.py:195
  33.8 22.6 %all_to_all.15 = bf16[16,48,384]{2,1,0:T(8,128)(2,1)S(1)} all-to-all(bf16[16,48,384]{2,1,0:T(8,128)(2,1)S(1)} %bitcast.8), channel_id=1, replica_groups={{0,2,4,6,64,66,68,70,128,130,132,134,192,194,196,198},{1,3,5,7,65,67,69..., dimensions={0} | all-to-all | bytes 1179648 | tf_op jit(solution)/shard_map/all_to_all | solution.py:181
  56.3 0.1 reduce_sum.24
  56.5 14.4 %all_to_all.16 = bf16[8,48,384]{2,1,0:T(8,128)(2,1)S(1)} all-to-all(bf16[8,48,384]{2,1,0:T(8,128)(2,1)S(1)} %broadcast_in_dim.7), channel_id=1, replica_groups={{0,8,16,24,32,40,48,56},{1,9,17,25,33,41,49,57},{2,10,18,26,34,42,50,58..., dimensions={0} | all-to-all | bytes 589824 | tf_op jit(solution)/shard_map/all_to_all | solution.py:181
  70.9 0.0 copy-start.3
  70.9 0.0 copy-start
  70.9 0.9 broadcast_in_dim.8
  71.8 4.4 %all-to-all-start.2 = ((bf16[16,48,384]{2,1,0:T(8,128)(2,1)}), bf16[16,48,384]{2,1,0:T(8,128)(2,1)S(1)}, u32[]{:S(2)}, u32[]{:S(2)}) async-start(bf16[16,48,384]{2,1,0:T(8,128)(2,1)} %broadcast_in_dim.8), calls=%async_computation.2 | async-start | bytes 1179648 | tf_op jit(solution)/shard_map/all_to_all | solution.py:181
  76.2 0.0 copy-done.3
  76.2 1.3 %collective-permute-start.2 = (bf16[4,128,384]{2,1,0:T(8,128)(2,1)S(1)}, bf16[4,128,384]{2,1,0:T(8,128)(2,1)S(1)}, u32[]{:S(2)}, u32[]{:S(2)}) collective-permute-start(bf16[4,128,384]{2,1,0:T(8,128)(2,1)S(1)} %copy-done.3), channel_id=1, source_target_pairs={{8,0},{16,8},{24,16},{32,24},{40,32},{48,40},{56,48},{64,56},{72,6... | collective-permute-start | bytes 1179656 | tf_op jit(solution)/shard_map/ppermute | solution.py:21
  77.5 8.0 %all-to-all-done.2 = bf16[16,48,384]{2,1,0:T(8,128)(2,1)S(1)} async-done(((bf16[16,48,384]{2,1,0:T(8,128)(2,1)}), bf16[16,48,384]{2,1,0:T(8,128)(2,1)S(1)}, u32[]{:S(2)}, u32[]{:S(2)}) %all-to-all-start.2) | async-done | bytes 589856 | tf_op jit(solution)/shard_map/all_to_all | solution.py:181
  85.5 4.7 %collective-permute-start.4 = (bf16[2,384,384]{2,1,0:T(8,128)(2,1)S(1)}, bf16[2,384,384]{2,1,0:T(8,128)(2,1)S(1)}, u32[]{:S(2)}, u32[]{:S(2)}) collective-permute-start(bf16[2,384,384]{2,1,0:T(8,128)(2,1)S(1)} %bitcast.6), channel_id=1, source_target_pairs={{0,1},{1,0},{2,3},{3,2},{4,5},{5,4},{6,7},{7,6},{8,9},{9,8},{10,11... | collective-permute-start | bytes 1769480 | tf_op jit(solution)/shard_map/ppermute | solution.py:177
  90.2 0.0 collective-permute-done.2
  90.2 0.0 copy-done
  90.2 0.8 add_convert_fusion.1
  91.0 0.8 collective-permute-done.4
  91.8 0.1 broadcast_select_fusion.1
  91.9 1.6 %maximum_convert_fusion = f32[4,384,384]{2,1,0:T(8,128)} fusion(bf16[2,384,384]{2,1,0:T(8,128)(2,1)S(1)} %get-tuple-element.14, bf16[2,384,384]{2,1,0:T(8,128)(2,1)S(1)} %get-tuple-element.13), kind=kLoop, calls=%fused_computation | loop fusion | flops 1179648 | bytes 3538944 | tf_op jit(solution)/shard_map/convert_element_type | solution.py:203
  (2 shorter events, 0.1 us)
Async XLA Ops:
  0.6 12.5 %collective-permute-start.1 = (bf16[4,128,384]{2,1,0:T(8,128)(2,1)}, bf16[4,128,384]{2,1,0:T(8,128)(2,1)S(1)}, u32[]{:S(2)}, u32[]{:S(2)}) collective-permute-start(bf16[4,128,384]{2,1,0:T(8,128)(2,1)} %x_ref.1), channel_id=1, source_target_pairs={{0,8},{8,16},{16,24},{24,32},{32,40},{40,48},{48,56},{56,64},{64,7... | collective-permute-start | bytes 1179656 | tf_op jit(solution)/shard_map/ppermute | solution.py:21
  5.0 8.1 %collective-permute-start = (s32[4,4]{1,0:T(4,128)}, s32[4,4]{1,0:T(4,128)S(1)}, u32[]{:S(2)}, u32[]{:S(2)}) collective-permute-start(s32[4,4]{1,0:T(4,128)} %own_counts.1), channel_id=1, source_target_pairs={{0,8},{8,16},{16,24},{24,32},{32,40},{40,48},{48,56},{56,64},{64,7... | collective-permute-start | bytes 200 | tf_op jit(solution)/shard_map/ppermute | solution.py:21
  13.1 0.6 copy-start.2
  13.1 0.7 copy-start.1
  28.1 4.2 %collective-permute-start.3 = (f32[2,384,384]{2,1,0:T(8,128)}, f32[2,384,384]{2,1,0:T(8,128)S(1)}, u32[]{:S(2)}, u32[]{:S(2)}) collective-permute-start(f32[2,384,384]{2,1,0:T(8,128)} %get-tuple-element.12), channel_id=1, source_target_pairs={{0,1},{1,0},{2,3},{3,2},{4,5},{5,4},{6,7},{7,6},{8,9},{9,8},{10,11... | collective-permute-start | bytes 3538952 | tf_op jit(solution)/shard_map/ppermute | solution.py:177
  70.9 5.3 %copy-start.3 = (bf16[4,128,384]{2,1,0:T(8,128)(2,1)S(1)}, bf16[4,128,384]{2,1,0:T(8,128)(2,1)}, u32[]{:S(2)}) copy-start(bf16[4,128,384]{2,1,0:T(8,128)(2,1)} %get-tuple-element.10) | copy-start | bytes 1179652
  70.9 19.3 %copy-start = (f32[4,128,384]{2,1,0:T(8,128)S(1)}, f32[4,128,384]{2,1,0:T(8,128)}, u32[]{:S(2)}) copy-start(f32[4,128,384]{2,1,0:T(8,128)} %get-tuple-element.9) | copy-start | bytes 2359300
  71.8 13.7 %all-to-all-start.2 = ((bf16[16,48,384]{2,1,0:T(8,128)(2,1)}), bf16[16,48,384]{2,1,0:T(8,128)(2,1)S(1)}, u32[]{:S(2)}, u32[]{:S(2)}) async-start(bf16[16,48,384]{2,1,0:T(8,128)(2,1)} %broadcast_in_dim.8), calls=%async_computation.2 | async-start | bytes 1179648 | tf_op jit(solution)/shard_map/all_to_all | solution.py:181
  76.2 14.0 %collective-permute-start.2 = (bf16[4,128,384]{2,1,0:T(8,128)(2,1)S(1)}, bf16[4,128,384]{2,1,0:T(8,128)(2,1)S(1)}, u32[]{:S(2)}, u32[]{:S(2)}) collective-permute-start(bf16[4,128,384]{2,1,0:T(8,128)(2,1)S(1)} %copy-done.3), channel_id=1, source_target_pairs={{8,0},{16,8},{24,16},{32,24},{40,32},{48,40},{56,48},{64,56},{72,6... | collective-permute-start | bytes 1179656 | tf_op jit(solution)/shard_map/ppermute | solution.py:21
  85.5 6.3 %collective-permute-start.4 = (bf16[2,384,384]{2,1,0:T(8,128)(2,1)S(1)}, bf16[2,384,384]{2,1,0:T(8,128)(2,1)S(1)}, u32[]{:S(2)}, u32[]{:S(2)}) collective-permute-start(bf16[2,384,384]{2,1,0:T(8,128)(2,1)S(1)} %bitcast.6), channel_id=1, source_target_pairs={{0,1},{1,0},{2,3},{3,2},{4,5},{5,4},{6,7},{7,6},{8,9},{9,8},{10,11... | collective-permute-start | bytes 1769480 | tf_op jit(solution)/shard_map/ppermute | solution.py:177

commit v2 on v1

--- a/solution.py
+++ b/solution.py
@@ -33,10 +33,36 @@
     return lax.dot_general(left, right, (((0,), (0,)), ((), ())), preferred_element_type=F32)
 
 
+def projection_kernel(x_ref, g_ref, wq_ref, wk_ref, wv_ref, wo_ref, q_ref, k_ref, v_ref, dc_ref):
+    batch, local, width = x_ref.shape
+    x = x_ref[...].reshape(batch * local, width)
+    g = g_ref[...].reshape(batch * local, width)
+
+    def spread(value):
+        return value.astype(BF16).reshape(batch, local, width)
+
+    q_ref[...] = spread(plain(x, wq_ref[...]))
+    k_ref[...] = spread(plain(x, wk_ref[...]))
+    v_ref[...] = spread(plain(x, wv_ref[...]))
+    dc_ref[...] = spread(rows_dot(g, wo_ref[...]))
+
+
+def projections(x, g, w_query, w_key, w_value, w_out):
+    vmem = pl.BlockSpec(memory_space=pltpu.VMEM)
+    return pl.pallas_call(
+        projection_kernel,
+        out_shape=[jax.ShapeDtypeStruct(x.shape, BF16)] * 4,
+        in_specs=[vmem] * 6,
+        out_specs=[vmem] * 4,
+        name="projections",
+    )(x, g, w_query, w_key, w_value, w_out)
+
+
 def attention_kernel(
-    own_counts, prev_counts, core_ref, x_ref, xp_ref, g_ref, wq_ref, wk_ref, wv_ref, wo_ref,
-    att_ref, fg_ref, fgp_ref, keep_ref, send_ref,
-    q_s, k_s, v_s, dc_s, ctx_s, dq_s, dk_s, dv_s,
+    own_counts, prev_counts, core_ref, q_hbm, k_hbm, v_hbm, dc_hbm, x_hbm, xp_hbm, g_hbm, wq_hbm, wk_hbm, wv_hbm, wo_hbm,
+    att_hbm, fg_hbm, fgp_hbm, keep_hbm, send_hbm,
+    x_ref, xp_ref, g_ref, wq_ref, wk_ref, wv_ref, wo_ref, att_ref, fg_ref, fgp_ref, grad_ref,
+    q_s, k_s, v_s, dc_s, ctx_s, dq_s, dk_s, dv_s, in_sem, out_sem,
 ):
     batch, local, width = x_ref.shape
     size = width // HEADS
@@ -44,20 +70,46 @@
     keys = CTX + local
     many = HEADS * local
     rows = batch * local
-
-    x = x_ref[...].reshape(rows, width)
-    xp = xp_ref[...].reshape(rows, width)
-    g = g_ref[...].reshape(rows, width)
+    core = core_ref[0]
+
+    own = pl.ds(CTX, local)
+    sources = [xp_hbm, wk_hbm, wv_hbm, q_hbm, k_hbm, v_hbm, dc_hbm, x_hbm, g_hbm, wo_hbm, wq_hbm]
+    targets = [xp_ref, wk_ref, wv_ref, q_s, k_s.at[:, own, :], v_s.at[:, own, :], dc_s, x_ref, g_ref, wo_ref, wq_ref]
+    loads = [pltpu.make_async_copy(s, t, in_sem.at[i]) for i, (s, t) in enumerate(zip(sources, targets))]
+    for load in loads:
+        load.start()
+
+    def grad_store(i, first):
+        out = keep_hbm if (i < 2) == first else send_hbm
+        return pltpu.make_async_copy(grad_ref.at[i], out.at[i % 2], out_sem.at[i])
+
+    def send_grad(i, value):
+        grad_ref[i] = value
+
+        @pl.when(core == 0)
+        def _():
+            grad_store(i, True).start()
+
+        @pl.when(core != 0)
+        def _():
+            grad_store(i, False).start()
+
+    stores = [
+        pltpu.make_async_copy(fg_ref, fg_hbm, out_sem.at[4]),
+        pltpu.make_async_copy(fgp_ref, fgp_hbm, out_sem.at[5]),
+        pltpu.make_async_copy(att_ref, att_hbm, out_sem.at[6]),
+    ]
 
     def spread(value):
         return value.astype(BF16).reshape(batch, local, width)
 
-    q_s[...] = spread(plain(x, wq_ref[...]))
-    dc_s[...] = spread(rows_dot(g, wo_ref[...]))
-    k_s[:, CTX:, :] = spread(plain(x, wk_ref[...]))
-    v_s[:, CTX:, :] = spread(plain(x, wv_ref[...]))
+    for load in loads[:3]:
+        load.wait()
+    xp = xp_ref[...].reshape(rows, width)
     k_s[:, :CTX, :] = spread(plain(xp, wk_ref[...]))
     v_s[:, :CTX, :] = spread(plain(xp, wv_ref[...]))
+    for load in loads[3:7]:
+        load.wait()
 
     head_of = lax.broadcasted_iota(jnp.int32, (local, width), 1) // size
     lane_span = (lax.broadcasted_iota(jnp.int32, (CH, many), 1) % local) // CH
@@ -99,8 +151,12 @@
         dv_s[u] = plain(probs_b, dcm).astype(BF16)
         return carry
 
-    lax.fori_loop(0, batch, one, 0)
-
+    lax.fori_loop(0, batch, one, 0, unroll=True)
+
+    for load in loads[7:]:
+        load.wait()
+    x = x_ref[...].reshape(rows, width)
+    g = g_ref[...].reshape(rows, width)
     ctx = ctx_s[...].reshape(rows, width)
     dq = dq_s[...].reshape(rows, width)
     dk = dk_s[:, CTX:, :].reshape(rows, width)
@@ -108,35 +164,39 @@
     dkp = dk_s[:, :CTX, :].reshape(rows, width)
     dvp = dv_s[:, :CTX, :].reshape(rows, width)
 
-    att_ref[...] = spread(plain(ctx, wo_ref[...]))
-    fgp_ref[...] = spread(rows_dot(dkp, wk_ref[...]) + rows_dot(dvp, wv_ref[...]))
+    send_grad(0, cols_dot(x, dq))
+    send_grad(1, cols_dot(x, dk) + cols_dot(xp, dkp))
+    send_grad(2, cols_dot(x, dv) + cols_dot(xp, dvp))
+    send_grad(3, cols_dot(ctx, g))
     total = rows_dot(dq, wq_ref[...]) + rows_dot(dk, wk_ref[...]) + rows_dot(dv, wv_ref[...])
     fg_ref[...] = total.reshape(batch, local, width)
-    grads = [
-        cols_dot(x, dq),
-        cols_dot(x, dk) + cols_dot(xp, dkp),
-        cols_dot(x, dv) + cols_dot(xp, dvp),
-        cols_dot(ctx, g),
-    ]
-    core = core_ref[0]
+    stores[0].start()
+    fgp_ref[...] = spread(rows_dot(dkp, wk_ref[...]) + rows_dot(dvp, wv_ref[...]))
+    stores[1].start()
+    att_ref[...] = spread(plain(ctx, wo_ref[...]))
+    stores[2].start()
 
     @pl.when(core == 0)
     def _():
-        for i in range(2):
-            keep_ref[i] = grads[i]
-            send_ref[i] = grads[2 + i]
+        for i in range(4):
+            grad_store(i, True).wait()
 
     @pl.when(core != 0)
     def _():
-        for i in range(2):
-            keep_ref[i] = grads[2 + i]
-            send_ref[i] = grads[i]
-
-
-def attention(own_counts, prev_counts, core, x, xp, g, w_query, w_key, w_value, w_out):
+        for i in range(4):
+            grad_store(i, False).wait()
+
+    for store in stores:
+        store.wait()
+
+
+def attention(own_counts, prev_counts, core, q, k, v, dc, x, xp, g, w_query, w_key, w_value, w_out):
     batch, local, width = x.shape
     smem = pl.BlockSpec(memory_space=pltpu.SMEM)
-    vmem = pl.BlockSpec(memory_space=pltpu.VMEM)
+    hbm = pl.BlockSpec(memory_space=pl.ANY)
+    weight = pltpu.VMEM((width, width), BF16)
+    wide = pltpu.VMEM((batch, local, width), F32)
+    grad = pltpu.VMEM((4, width, width), F32)
     short = pltpu.VMEM((batch, local, width), BF16)
     long = pltpu.VMEM((batch, CTX + local, width), BF16)
     return pl.pallas_call(
@@ -148,11 +208,13 @@
             jax.ShapeDtypeStruct((2, width, width), F32),
             jax.ShapeDtypeStruct((2, width, width), F32),
         ],
-        in_specs=[smem] * 3 + [vmem] * 7,
-        out_specs=[vmem] * 5,
-        scratch_shapes=[short, long, long, short, short, short, long, long],
+        in_specs=[smem] * 3 + [hbm] * 11,
+        out_specs=[hbm] * 5,
+        scratch_shapes=[short] * 3 + [weight] * 4 + [short, wide, short, grad]
+        + [short, long, long, short, short, short, long, long]
+        + [pltpu.SemaphoreType.DMA((11,)), pltpu.SemaphoreType.DMA((7,))],
         name="attention",
-    )(own_counts, prev_counts, core, x, xp, g, w_query, w_key, w_value, w_out)
+    )(own_counts, prev_counts, core, q, k, v, dc, x, xp, g, w_query, w_key, w_value, w_out)
 
 
 def groups():
@@ -207,8 +269,9 @@
     core = lax.axis_index("dp") % CORES
     prev_frames = shifted(frames, "seq", 1)
     prev_counts = shifted(valid_counts, "seq", 1)
+    local = projections(frames, out_grad, w_query, w_key, w_value, w_out)
     attended, own, back, keep, send = attention(
-        valid_counts, prev_counts, core[None], frames, prev_frames, out_grad, w_query, w_key, w_value, w_out
+        valid_counts, prev_counts, core[None], *local, frames, prev_frames, out_grad, w_query, w_key, w_value, w_out
     )
     returned = shifted(back, "seq", -1)
     weight_grads = total_grads(keep, send, core)

time: 93.9 us -> 91.6 us (0.976)
  waiting for transfers between devices: 16 us -> 12.7 us
  Pallas kernels: 14.2 us -> 15.2 us
    ppermute x3, waiting for transfers between devices: 4.52 us -> 1.18 us  [shifted(): return lax.ppermute(value, axis, pairs)]
    pallas_call x0 -> x1, Pallas kernels: none -> 3.34 us  [projections(): pl.pallas_call(projection_kernel, out_shape=[jax.ShapeDtypeStruct(x.shape...]
    pallas_call x1, Pallas kernels: 14.2 us -> 11.8 us  [attention(): pl.pallas_call(attention_kernel, out_shape=[jax.ShapeDtypeStruct((batch,...]
  transfers between devices with their start and end apart: 6 -> 6, of which waited for: 4 -> 4; matrix products, arithmetic and copies ran while one was open for 1% -> 1% of each run, Pallas kernels for 0% -> 4%
where the time goes in v2:
time: 91.6 us; the launch traced here: 91.2 us
  blocking collectives  37 us (40%)
  starting transfers between devices  19.9 us (22%)
  Pallas kernels  15.2 us (17%)
  waiting for transfers between devices  12.7 us (14%)
  other arithmetic  4.08 us (4%)
  local copies, waits for them, and re-layouts  1.65 us (2%)
    all_to_all x2, blocking collectives, exchange(): return lax.all_to_all(value, EVERY, 0, 0, axis_index_groups=members)  37 us
    pallas_call x1, Pallas kernels, attention(): pl.pallas_call(attention_kernel, out_shape=[jax.ShapeDtypeStruct((batch,...  11.8 us
    ppermute x3, starting transfers between devices, shifted(): return lax.ppermute(value, axis, pairs)  9.21 us
    all_to_all x1, waiting for transfers between devices, exchange(): return lax.all_to_all(value, EVERY, 0, 0, axis_index_groups=members)  8.03 us
    ppermute x2, starting transfers between devices, partner(): return lax.ppermute(value, 'dp', pairs)  6.34 us
    all_to_all x1, starting transfers between devices, exchange(): return lax.all_to_all(value, EVERY, 0, 0, axis_index_groups=members)  4.37 us
    ppermute x2, waiting for transfers between devices, partner(): return lax.ppermute(value, 'dp', pairs)  3.49 us
    pallas_call x1, Pallas kernels, projections(): pl.pallas_call(projection_kernel, out_shape=[jax.ShapeDtypeStruct(x.shape...  3.34 us
  transfers between devices with their start and end apart: 6, of which 4 were waited for; matrix products, arithmetic and copies ran while one was open for 1% of the time, Pallas kernels for 4%

profile of v2, /device:TPU:1, one launch (start us, length us, event | category | flops | bytes accessed | tf_op | source)
XLA Modules:
  0.0 91.2 jit_solution(18059533496593194306)
XLA Ops:
  0.6 4.4 %collective-permute-start.1 = (bf16[4,128,384]{2,1,0:T(8,128)(2,1)}, bf16[4,128,384]{2,1,0:T(8,128)(2,1)S(1)}, u32[]{:S(2)}, u32[]{:S(2)}) collective-permute-start(bf16[4,128,384]{2,1,0:T(8,128)(2,1)} %x_hbm.1), channel_id=1, source_target_pairs={{0,8},{8,16},{16,24},{24,32},{32,40},{40,48},{48,56},{56,64},{64,7... | collective-permute-start | bytes 1179656 | tf_op jit(solution)/shard_map/ppermute | solution.py:21
  5.0 3.5 %collective-permute-start = (s32[4,4]{1,0:T(4,128)}, s32[4,4]{1,0:T(4,128)S(1)}, u32[]{:S(2)}, u32[]{:S(2)}) collective-permute-start(s32[4,4]{1,0:T(4,128)} %own_counts.1), channel_id=1, source_target_pairs={{0,8},{8,16},{16,24},{24,32},{32,40},{40,48},{48,56},{56,64},{64,7... | collective-permute-start | bytes 200 | tf_op jit(solution)/shard_map/ppermute | solution.py:21
  8.6 3.3 %projections.1 = (bf16[4,128,384]{2,1,0:T(8,128)(2,1)}, bf16[4,128,384]{2,1,0:T(8,128)(2,1)}, bf16[4,128,384]{2,1,0:T(8,128)(2,1)}, bf16[4,128,384]{2,1,0:T(8,128)(2,1)}) custom-call(bf16[4,128,384]{2,1,0:T(8,128)(2,1)} %x_hbm.1, bf16[4,128,384]{2,1,0:T(8,128)(2,1)} %g_hbm.1, bf16[384,384]{1,0:T(8,128)(2,1)} %wq_hbm.1, bf16[384,384]{1,0:T(8,128)(2,1)} %wk_hbm.1, ...), custom_call_target="tpu_custom_call" | custom-call | tf_op jit(solution)/shard_map/projections/pallas_call | solution.py:52
  11.9 1.2 %collective-permute-done.prev_counts = s32[4,4]{1,0:T(4,128)S(1)} collective-permute-done((s32[4,4]{1,0:T(4,128)}, s32[4,4]{1,0:T(4,128)S(1)}, u32[]{:S(2)}, u32[]{:S(2)}) %collective-permute-start) | collective-permute-done | bytes 96 | tf_op jit(solution)/shard_map/ppermute | solution.py:21
  13.1 0.0 copy-start.2
  13.1 0.0 collective-permute-done.1.xp_hbm
  13.1 0.0 copy-start.1
  13.1 0.6 copy-done.2
  13.7 0.2 copy-done.1
  13.8 11.8 %attention.1 = (bf16[4,128,384]{2,1,0:T(8,128)(2,1)}, f32[4,128,384]{2,1,0:T(8,128)}, bf16[4,128,384]{2,1,0:T(8,128)(2,1)}, f32[2,384,384]{2,1,0:T(8,128)}, f32[2,384,384]{2,1,0:T(8,128)}) custom-call(s32[4,4]{1,0:T(4,128)} %own_counts.1, s32[4,4]{1,0:T(4,128)} %copy-done.2, s32[1]{0:T(128)} %bitcast.core_ref, bf16[4,128,384]{2,1,0:T(8,128)(2,1)} %get-tuple-element.12.q_hbm, ...), custom_call_target="tpu_custom_call" | custom-call | tf_op jit(solution)/shard_map/attention/pallas_call | solution.py:202
  25.7 1.7 %collective-permute-start.3 = (f32[2,384,384]{2,1,0:T(8,128)}, f32[2,384,384]{2,1,0:T(8,128)S(1)}, u32[]{:S(2)}, u32[]{:S(2)}) collective-permute-start(f32[2,384,384]{2,1,0:T(8,128)} %get-tuple-element.20), channel_id=1, source_target_pairs={{0,1},{1,0},{2,3},{3,2},{4,5},{5,4},{6,7},{7,6},{8,9},{9,8},{10,11... | collective-permute-start | bytes 3538952 | tf_op jit(solution)/shard_map/ppermute | solution.py:239
  27.3 2.7 %collective-permute-done.3 = f32[2,384,384]{2,1,0:T(8,128)S(1)} collective-permute-done((f32[2,384,384]{2,1,0:T(8,128)}, f32[2,384,384]{2,1,0:T(8,128)S(1)}, u32[]{:S(2)}, u32[]{:S(2)}) %collective-permute-start.3) | collective-permute-done | bytes 1179680 | tf_op jit(solution)/shard_map/ppermute | solution.py:239
  30.0 1.5 %add_convert_fusion = bf16[2,384,384]{2,1,0:T(8,128)(2,1)S(1)} fusion(f32[2,384,384]{2,1,0:T(8,128)} %get-tuple-element.19, f32[2,384,384]{2,1,0:T(8,128)S(1)} %collective-permute-done.3), kind=kLoop, calls=%fused_computation.1 | loop fusion | flops 589824 | bytes 2949120 | tf_op jit(solution)/shard_map/convert_element_type | solution.py:257
  31.5 22.6 %all_to_all.15 = bf16[16,48,384]{2,1,0:T(8,128)(2,1)S(1)} all-to-all(bf16[16,48,384]{2,1,0:T(8,128)(2,1)S(1)} %bitcast.8), channel_id=1, replica_groups={{0,2,4,6,64,66,68,70,128,130,132,134,192,194,196,198},{1,3,5,7,65,67,69..., dimensions={0} | all-to-all | bytes 1179648 | tf_op jit(solution)/shard_map/all_to_all | solution.py:243
  54.1 0.1 reduce_sum.24
  54.2 14.4 %all_to_all.16 = bf16[8,48,384]{2,1,0:T(8,128)(2,1)S(1)} all-to-all(bf16[8,48,384]{2,1,0:T(8,128)(2,1)S(1)} %broadcast_in_dim.7), channel_id=1, replica_groups={{0,8,16,24,32,40,48,56},{1,9,17,25,33,41,49,57},{2,10,18,26,34,42,50,58..., dimensions={0} | all-to-all | bytes 589824 | tf_op jit(solution)/shard_map/all_to_all | solution.py:243
  68.6 0.0 copy-start.3
  68.6 0.0 copy-start
  68.6 0.9 broadcast_in_dim.8
  69.5 4.4 %all-to-all-start.2 = ((bf16[16,48,384]{2,1,0:T(8,128)(2,1)}), bf16[16,48,384]{2,1,0:T(8,128)(2,1)S(1)}, u32[]{:S(2)}, u32[]{:S(2)}) async-start(bf16[16,48,384]{2,1,0:T(8,128)(2,1)} %broadcast_in_dim.8), calls=%async_computation.2 | async-start | bytes 1179648 | tf_op jit(solution)/shard_map/all_to_all | solution.py:243
  73.9 0.0 copy-done.3
  73.9 1.3 %collective-permute-start.2 = (bf16[4,128,384]{2,1,0:T(8,128)(2,1)S(1)}, bf16[4,128,384]{2,1,0:T(8,128)(2,1)S(1)}, u32[]{:S(2)}, u32[]{:S(2)}) collective-permute-start(bf16[4,128,384]{2,1,0:T(8,128)(2,1)S(1)} %copy-done.3), channel_id=1, source_target_pairs={{8,0},{16,8},{24,16},{32,24},{40,32},{48,40},{56,48},{64,56},{72,6... | collective-permute-start | bytes 1179656 | tf_op jit(solution)/shard_map/ppermute | solution.py:21
  75.2 8.0 %all-to-all-done.2 = bf16[16,48,384]{2,1,0:T(8,128)(2,1)S(1)} async-done(((bf16[16,48,384]{2,1,0:T(8,128)(2,1)}), bf16[16,48,384]{2,1,0:T(8,128)(2,1)S(1)}, u32[]{:S(2)}, u32[]{:S(2)}) %all-to-all-start.2) | async-done | bytes 589856 | tf_op jit(solution)/shard_map/all_to_all | solution.py:243
  83.2 4.7 %collective-permute-start.4 = (bf16[2,384,384]{2,1,0:T(8,128)(2,1)S(1)}, bf16[2,384,384]{2,1,0:T(8,128)(2,1)S(1)}, u32[]{:S(2)}, u32[]{:S(2)}) collective-permute-start(bf16[2,384,384]{2,1,0:T(8,128)(2,1)S(1)} %bitcast.6), channel_id=1, source_target_pairs={{0,1},{1,0},{2,3},{3,2},{4,5},{5,4},{6,7},{7,6},{8,9},{9,8},{10,11... | collective-permute-start | bytes 1769480 | tf_op jit(solution)/shard_map/ppermute | solution.py:239
  87.9 0.0 collective-permute-done.2
  87.9 0.0 copy-done
  87.9 0.8 add_convert_fusion.1
  88.7 0.8 collective-permute-done.4
  89.5 0.1 broadcast_select_fusion.1
  89.7 1.6 %maximum_convert_fusion = f32[4,384,384]{2,1,0:T(8,128)} fusion(bf16[2,384,384]{2,1,0:T(8,128)(2,1)S(1)} %get-tuple-element.22, bf16[2,384,384]{2,1,0:T(8,128)(2,1)S(1)} %get-tuple-element.21), kind=kLoop, calls=%fused_computation | loop fusion | flops 1179648 | bytes 3538944 | tf_op jit(solution)/shard_map/convert_element_type | solution.py:265
  (2 shorter events, 0.1 us)
Async XLA Ops:
  0.6 12.5 %collective-permute-start.1 = (bf16[4,128,384]{2,1,0:T(8,128)(2,1)}, bf16[4,128,384]{2,1,0:T(8,128)(2,1)S(1)}, u32[]{:S(2)}, u32[]{:S(2)}) collective-permute-start(bf16[4,128,384]{2,1,0:T(8,128)(2,1)} %x_hbm.1), channel_id=1, source_target_pairs={{0,8},{8,16},{16,24},{24,32},{32,40},{40,48},{48,56},{56,64},{64,7... | collective-permute-start | bytes 1179656 | tf_op jit(solution)/shard_map/ppermute | solution.py:21
  5.0 8.1 %collective-permute-start = (s32[4,4]{1,0:T(4,128)}, s32[4,4]{1,0:T(4,128)S(1)}, u32[]{:S(2)}, u32[]{:S(2)}) collective-permute-start(s32[4,4]{1,0:T(4,128)} %own_counts.1), channel_id=1, source_target_pairs={{0,8},{8,16},{16,24},{24,32},{32,40},{40,48},{48,56},{56,64},{64,7... | collective-permute-start | bytes 200 | tf_op jit(solution)/shard_map/ppermute | solution.py:21
  13.1 0.6 copy-start.2
  13.1 0.7 copy-start.1
  25.7 4.3 %collective-permute-start.3 = (f32[2,384,384]{2,1,0:T(8,128)}, f32[2,384,384]{2,1,0:T(8,128)S(1)}, u32[]{:S(2)}, u32[]{:S(2)}) collective-permute-start(f32[2,384,384]{2,1,0:T(8,128)} %get-tuple-element.20), channel_id=1, source_target_pairs={{0,1},{1,0},{2,3},{3,2},{4,5},{5,4},{6,7},{7,6},{8,9},{9,8},{10,11... | collective-permute-start | bytes 3538952 | tf_op jit(solution)/shard_map/ppermute | solution.py:239
  68.6 5.3 %copy-start.3 = (bf16[4,128,384]{2,1,0:T(8,128)(2,1)S(1)}, bf16[4,128,384]{2,1,0:T(8,128)(2,1)}, u32[]{:S(2)}) copy-start(bf16[4,128,384]{2,1,0:T(8,128)(2,1)} %get-tuple-element.18) | copy-start | bytes 1179652
  68.6 19.3 %copy-start = (f32[4,128,384]{2,1,0:T(8,128)S(1)}, f32[4,128,384]{2,1,0:T(8,128)}, u32[]{:S(2)}) copy-start(f32[4,128,384]{2,1,0:T(8,128)} %get-tuple-element.17) | copy-start | bytes 2359300
  69.5 13.7 %all-to-all-start.2 = ((bf16[16,48,384]{2,1,0:T(8,128)(2,1)}), bf16[16,48,384]{2,1,0:T(8,128)(2,1)S(1)}, u32[]{:S(2)}, u32[]{:S(2)}) async-start(bf16[16,48,384]{2,1,0:T(8,128)(2,1)} %broadcast_in_dim.8), calls=%async_computation.2 | async-start | bytes 1179648 | tf_op jit(solution)/shard_map/all_to_all | solution.py:243
  73.9 14.0 %collective-permute-start.2 = (bf16[4,128,384]{2,1,0:T(8,128)(2,1)S(1)}, bf16[4,128,384]{2,1,0:T(8,128)(2,1)S(1)}, u32[]{:S(2)}, u32[]{:S(2)}) collective-permute-start(bf16[4,128,384]{2,1,0:T(8,128)(2,1)S(1)} %copy-done.3), channel_id=1, source_target_pairs={{8,0},{16,8},{24,16},{32,24},{40,32},{48,40},{56,48},{64,56},{72,6... | collective-permute-start | bytes 1179656 | tf_op jit(solution)/shard_map/ppermute | solution.py:21
  83.2 6.3 %collective-permute-start.4 = (bf16[2,384,384]{2,1,0:T(8,128)(2,1)S(1)}, bf16[2,384,384]{2,1,0:T(8,128)(2,1)S(1)}, u32[]{:S(2)}, u32[]{:S(2)}) collective-permute-start(bf16[2,384,384]{2,1,0:T(8,128)(2,1)S(1)} %bitcast.6), channel_id=1, source_target_pairs={{0,1},{1,0},{2,3},{3,2},{4,5},{5,4},{6,7},{7,6},{8,9},{9,8},{10,11... | collective-permute-start | bytes 1769480 | tf_op jit(solution)/shard_map/ppermute | solution.py:239
